TPU v7x, 32 devices: a whole 2x2x4 slice. The times are simulated.
32 devices in a mesh: row: 4 (over z), col: 8 (over y, x, core).
Axes of the slice: x: 2, y: 2, z: 4, core: 2. Of those that a mesh axis runs over, the one named last changes fastest.
Arguments:
- splat_params: float32 [10, 2097152], P(None, ('row', 'col')), as said below
- list_owner: int32 [128, 1024, 1], P(('row', 'col')), may hold values from 0 to 31; in each aligned block of 4096 rows (0 to 4095, 4096 to 8191, ..., all dimensions but the last counted through in order) at most 256 rows name the same one
- list_slot: int32 [128, 1024], P(('row', 'col')), may hold values from 0 to 65535
- list_length: int32 [128], P(('row', 'col')), may hold values from 512 to 1024, as said below
- target: float32 [4, 128, 256], P(None, ('row', 'col')), may hold values from 0 to 1
Outputs:
- rendered: float32 [4, 128, 256], P(None, ('row', 'col'))
- splat_grads: float32 [10, 2097152], P(None, ('row', 'col'))
Inputs may be any that keep to these rules, and one draw needn't show every extreme that they name: `list_owner`: within the entries of one device's tiles (aligned blocks of 4096 entries), no owner is named more than 256 times, a bound that some block reaches. `list_length`: some tile has exactly 1024 live entries; every tile has at least 512. `splat_params`: conic entries satisfy a > 0, c > 0 and b * b < a * c; opacity lies in (0, 0.02]; colours and depth lie in [0, 1].
All inputs are finite; a program needn't handle non-finite values.
Results may differ from a plain program's by a relative error of at most 0.0003.
Values sent between devices are 32-bit elements; how exact they have to be, the bound alone decides.
A program may use at most 128 MiB of HBM per device.

v0:
```python
import functools

import jax
import jax.numpy as jnp
from jax import lax
from jax.experimental import pallas as pl
from jax.experimental.pallas import tpu as pltpu
from jax.sharding import PartitionSpec as P

SIDE = 16
SB = 256
CH = 10
F32 = jnp.float32
BF16 = jnp.bfloat16
NT = (((1,), (1,)), ((), ()))
BLOCK = 512
LOG2E = 1.4426950408889634


def iota(shape, dim):
    return lax.broadcasted_iota(jnp.int32, shape, dim)


def split(x):
    high = x.astype(BF16)
    return high, (x - high.astype(F32)).astype(BF16)


def mm(a, b):
    return jnp.dot(a, b, preferred_element_type=F32)


def mm_nt(a, b):
    return lax.dot_general(a, b, NT, preferred_element_type=F32)


def one_hot(index, size):
    return jnp.where(iota((size, index.shape[1]), 0) == index, 1.0, 0.0).astype(BF16)


def step_kernel(
    length_ref, own_ref, slot_ref, target_ref, params_hbm, image_ref, asked_ref, incoming_ref, coming_ref,
    params_ref, table_ref, wide_ref, even_ref, odd_ref, lines_ref, live_ref, rank_ref, req_ref,
    found_ref, find_ref, replies_ref, reply_ref, outgoing_ref, going_ref, reply_both, sent_ref,
    vals, grads, falloff_ref, trans_ref, both_ref, shade_ref, after_ref, pack_ref, heavy_ref, light_ref,
    local_sem, send_sem, recv_sem,
):
    rows_on = lax.axis_size("row")
    cols_on = lax.axis_size("col")
    devices = rows_on * cols_on
    me = lax.axis_index("row") * cols_on + lax.axis_index("col")
    tiles, slots = slot_ref.shape
    cap = found_ref.shape[2]
    pixels = target_ref.shape[2]
    rows = table_ref.shape[0]
    others = pl.ds(0, devices - 1)

    def peer(k):
        return lax.rem(me + k, devices)

    def place_of(device):
        return (device // cols_on, lax.rem(device, cols_on))

    def push(device, source, target, phase):
        return pltpu.make_async_remote_copy(
            src_ref=source.at[device],
            dst_ref=target.at[me],
            send_sem=send_sem.at[phase],
            recv_sem=recv_sem.at[phase],
            device_id=place_of(device),
            device_id_type=pl.DeviceIdType.MESH,
        )

    def drain(source, target, phase):
        pltpu.make_async_copy(target.at[others], target.at[others], recv_sem.at[phase]).wait()
        pltpu.make_async_copy(source.at[others], source.at[others], send_sem.at[phase]).wait()

    barrier = pltpu.get_barrier_semaphore()

    @pl.loop(1, devices)
    def _(k):
        pl.semaphore_signal(
            barrier, inc=1, device_id=place_of(peer(k)), device_id_type=pl.DeviceIdType.MESH
        )

    load = pltpu.make_async_copy(params_hbm, params_ref, local_sem.at[0])
    load.start()

    strict = jnp.where(iota((SB, SB), 0) < iota((SB, SB), 1), 1.0, 0.0).astype(BF16)
    later = jnp.where(iota((SB, SB), 0) > iota((SB, SB), 1), 1.0, 0.0).astype(BF16)
    strict_twice = jnp.concatenate([strict, strict], axis=0)
    later_twice = jnp.concatenate([later, later], axis=0)
    count = jnp.zeros((devices, 1), F32)
    high = jnp.zeros((devices, cap), F32)
    low = jnp.zeros((devices, cap), F32)
    for tile in range(tiles):
        for j in range(slots // SB):
            part = slice(j * SB, (j + 1) * SB)
            owner = jnp.where(iota((1, SB), 1) + j * SB < length_ref[tile], own_ref[tile, :, part], -1)
            live_ref[tile, :, part] = owner
            mine = iota((devices, SB), 0) == owner
            ones = jnp.where(mine, 1.0, 0.0)
            ahead = mm(ones.astype(BF16), strict) + count
            rank = jnp.sum(ones * ahead, axis=0, keepdims=True).astype(jnp.int32)
            count = count + jnp.sum(ones, axis=1, keepdims=True)
            rank_ref[tile, :, part] = rank
            named = slot_ref[tile : tile + 1, part]
            places = one_hot(rank, cap)
            slot_high = (named >> 8).astype(F32)
            slot_low = ((named & 255) + 1).astype(F32)
            high = high + mm_nt(jnp.where(mine, slot_high, 0.0).astype(BF16), places)
            low = low + mm_nt(jnp.where(mine, slot_low, 0.0).astype(BF16), places)
    wanted = (high * 256.0 + low).astype(jnp.int32) - 1
    chunk = wanted >> (8 * BLOCK).bit_length() - 1
    line = (chunk & (rows // BLOCK - 1)) * BLOCK + (wanted & (BLOCK - 1))
    group = jnp.where(wanted < 0, -1, (wanted >> BLOCK.bit_length() - 1) & 7)
    filled = jnp.broadcast_to(count, (devices, 128)).astype(jnp.int32)
    for d in range(devices):
        req_ref[d, :, :cap] = line[d : d + 1]
        req_ref[d, :, cap : 2 * cap] = group[d : d + 1]
        req_ref[d, :, 2 * cap :] = filled[d : d + 1]
    pl.semaphore_wait(barrier, devices - 1)

    @pl.loop(1, devices)
    def _(k):
        push(peer(k), req_ref, asked_ref, 0).start()

    asked_ref[me] = req_ref[me]
    load.wait()
    wide_ref[...] = jnp.zeros_like(wide_ref)

    @pl.loop(0, rows // BLOCK)
    def _(j):
        for k in range(8):
            at = pl.ds(pl.multiple_of((j * 8 + k) * BLOCK, BLOCK), BLOCK)
            wide_ref[k * 16 : k * 16 + CH, :] = params_ref[:, at]
        table_ref[pl.ds(pl.multiple_of(j * BLOCK, BLOCK), BLOCK), :] = jnp.transpose(wide_ref[...])

    drain(req_ref, asked_ref, 0)
    move = pltpu.make_async_copy(asked_ref, lines_ref, local_sem.at[1])
    move.start()
    move.wait()

    eye = jnp.where(iota((128, 128), 0) == iota((128, 128), 1), 1.0, 0.0).astype(BF16)

    def fetch(source, held):
        for j in range(cap):
            held[j : j + 1, :] = table_ref[pl.ds(lines_ref[source, 0, j], 1), :]

    def pick(source, held):
        high, low = split(held[...])
        turned = mm_nt(eye, high) + mm_nt(eye, low)
        group = asked_ref[source, :, cap : 2 * cap]
        found = jnp.zeros((16, cap), F32)
        for q in range(8):
            found = found + jnp.where(group == q, turned[q * 16 : q * 16 + 16], 0.0)
        return found[:8], found[8:CH]

    def answer(source, held):
        found_ref[source], find_ref[source] = pick(source, held)
        push(source, found_ref, replies_ref, 1).start()
        push(source, find_ref, reply_ref, 2).start()

    fetch(peer(1), even_ref)

    @pl.loop(0, devices // 2 - 1)
    def _(p):
        fetch(peer(2 * p + 2), odd_ref)
        answer(peer(2 * p + 1), even_ref)
        fetch(peer(2 * p + 3), even_ref)
        answer(peer(2 * p + 2), odd_ref)

    answer(peer(devices - 1), even_ref)
    fetch(me, odd_ref)
    replies_ref[me], reply_ref[me] = pick(me, odd_ref)
    drain(found_ref, replies_ref, 1)
    drain(find_ref, reply_ref, 2)

    for ch in range(CH):
        part = slice(ch * devices, (ch + 1) * devices)
        reply_both[part, :cap], reply_both[part, cap:] = split(replies_ref[:, ch, :] if ch < 8 else reply_ref[:, ch - 8, :])
    sent_ref[...] = jnp.zeros_like(sent_ref)
    blocks = slots // SB
    centres = iota((SIDE, SB), 0).astype(F32) + 0.5
    side_rows = pixels // SIDE

    @pl.loop(0, tiles)
    def _(tile):
        length = length_ref[tile]
        mine = iota((devices, slots), 0) == live_ref[tile]
        places = one_hot(rank_ref[tile], cap)
        fetched = mm(reply_both[...], jnp.concatenate([places, places], axis=0))
        vals[...] = jnp.zeros_like(vals)
        live = jnp.where(iota((1, slots), 1) < length, 1.0, 0.0)
        for ch in range(CH):
            part = slice(ch * devices, (ch + 1) * devices)
            value = jnp.sum(jnp.where(mine, fetched[part], 0.0), axis=0, keepdims=True)
            if ch == 5:
                value = value * live
            row = ch if ch < 6 else ch + 2
            vals[row : row + 1, :] = value

        carry = jnp.zeros((pixels, 1), F32)
        image = jnp.zeros((pixels, 16), F32)
        image_light = jnp.zeros((pixels, 8), F32)
        for blk in range(blocks):
            at = slice(blk * SB, (blk + 1) * SB)
            dx = centres - vals[0:1, at]
            dy = centres - vals[1:2, at]
            ex = (-0.5 * LOG2E) * vals[2:3, at] * dx * dx
            ey = (-0.5 * LOG2E) * vals[4:5, at] * dy * dy
            bdy = -LOG2E * vals[3:4, at] * dy
            opacity = vals[5:6, at]
            for y in range(side_rows):
                rows_at = slice(y * SIDE, (y + 1) * SIDE)
                falloff = jnp.exp2(ex + ey[y : y + 1] + dx * bdy[y : y + 1])
                falloff_ref[rows_at, at] = falloff
                both_ref[rows_at, :SB], both_ref[rows_at, SB:] = split(jnp.log2(1.0 - opacity * falloff))
            total = mm(both_ref[...], strict_twice) + carry
            last = both_ref[:, SB - 128 : SB].astype(F32) + both_ref[:, 2 * SB - 128 :].astype(F32)
            carry = total[:, SB - 1 : SB] + last[:, 127:128]
            trans = jnp.exp2(total)
            trans_ref[:, at] = trans
            weight_high, weight_low = split(trans * (opacity * falloff_ref[:, at]))
            heavy_ref[:, at] = weight_high
            light_ref[:, at] = weight_low
            colour_high, colour_low = split(vals[8:16, at])
            image = image + mm_nt(weight_high, jnp.concatenate([colour_high, colour_low], axis=0))
            image_light = image_light + mm_nt(weight_low, colour_high)
        turned_image = jnp.transpose(image)
        rendered = turned_image[:8] + turned_image[8:] + jnp.transpose(image_light)
        for ch in range(4):
            image_ref[ch, pl.ds(tile, 1), :] = rendered[ch : ch + 1]
        wished = [target_ref[ch, pl.ds(tile, 1), :] for ch in range(4)]
        wished = jnp.concatenate(wished + [jnp.zeros((4, pixels), F32)], axis=0)
        grad_image = 2.0 * (rendered - wished)
        grad_high, grad_low = split(grad_image)
        grad_wide = grad_high.astype(F32)
        grad_rest = grad_image - grad_wide
        turned = jnp.transpose(jnp.concatenate([grad_wide, grad_wide, grad_rest, grad_image], axis=0))
        turned_parts = turned.astype(BF16)
        grad_both = jnp.concatenate([grad_high, grad_low], axis=0)

        spent = jnp.zeros((pixels, 1), F32)
        for blk in reversed(range(blocks)):
            at = slice(blk * SB, (blk + 1) * SB)
            mean_x, mean_y = vals[0:1, at], vals[1:2, at]
            conic_a, conic_b, conic_c = vals[2:3, at], vals[3:4, at], vals[4:5, at]
            opacity = vals[5:6, at]
            dx = centres - mean_x
            dy = centres - mean_y
            colours = vals[8:16, at]
            colour_wide = colours.astype(BF16).astype(F32)
            colour_parts = jnp.concatenate(
                [colour_wide, colours - colour_wide, colour_wide, jnp.zeros_like(colours)], axis=0
            ).astype(BF16)
            shading = mm(turned_parts, colour_parts)
            shade_ref[...] = shading
            colour_grads = mm(grad_both, heavy_ref[:, at])
            grads[8:16, at] = colour_grads[:8] + colour_grads[8:] + mm(grad_high, light_ref[:, at])
            gain = trans_ref[:, at] * (opacity * falloff_ref[:, at]) * shading
            both_ref[:, :SB], both_ref[:, SB:] = split(gain)
            after = mm(both_ref[...], later_twice) + spent
            spent = after[:, 0:1] + gain[:, 0:1]
            after_ref[...] = after
            moment0 = jnp.zeros((SIDE, SB), F32)
            moment1 = moment0
            moment2 = moment0
            for y in range(side_rows):
                rows_at = slice(y * SIDE, (y + 1) * SIDE)
                falloff = falloff_ref[rows_at, at]
                grad_alpha = trans_ref[rows_at, at] * shade_ref[rows_at, :] - after_ref[rows_at, :] / (
                    1.0 - opacity * falloff
                )
                opaque = grad_alpha * falloff
                moment0 = moment0 + opaque
                lever = opaque * dy[y : y + 1]
                moment1 = moment1 + lever
                moment2 = moment2 + lever * dy[y : y + 1]
            across = moment0 * dx
            sum_x = jnp.sum(across, axis=0, keepdims=True)
            sum_y = jnp.sum(moment1, axis=0, keepdims=True)
            grads[0:1, at] = opacity * (conic_a * sum_x + conic_b * sum_y)
            grads[1:2, at] = opacity * (conic_c * sum_y + conic_b * sum_x)
            grads[2:3, at] = -0.5 * opacity * jnp.sum(across * dx, axis=0, keepdims=True)
            grads[3:4, at] = -opacity * jnp.sum(moment1 * dx, axis=0, keepdims=True)
            grads[4:5, at] = -0.5 * opacity * jnp.sum(moment2, axis=0, keepdims=True)
            grads[5:6, at] = jnp.sum(moment0, axis=0, keepdims=True) * live[:, at]

        for ch in range(CH):
            part = slice(ch * devices, (ch + 1) * devices)
            row = ch if ch < 6 else ch + 2
            high, low = split(jnp.where(mine, grads[row : row + 1, :], 0.0))
            pack_ref[part, :slots] = high
            pack_ref[part, slots:] = low
        sent = mm_nt(pack_ref[...], jnp.concatenate([places, places], axis=1))

        sent_ref[...] += sent

    for ch in range(CH):
        part = slice(ch * devices, (ch + 1) * devices)
        if ch < 8:
            outgoing_ref[:, ch, :] = sent_ref[part, :]
        else:
            going_ref[:, ch - 8, :] = sent_ref[part, :]

    @pl.loop(1, devices)
    def _(k):
        push(peer(k), outgoing_ref, incoming_ref, 3).start()
        push(peer(k), going_ref, coming_ref, 4).start()

    incoming_ref[me] = outgoing_ref[me]
    coming_ref[me] = going_ref[me]
    drain(outgoing_ref, incoming_ref, 3)
    drain(going_ref, coming_ref, 4)


def scatter_kernel(
    line_ref, ask_ref, grad_ref, rest_ref, out_hbm, wide_ref, out_ref, out_sem, *banks
):
    rows = banks[0].shape[0]
    devices, _, cap = grad_ref.shape
    share = rows // devices
    burst = 32

    @pl.loop(0, devices // 2)
    def _(p):
        wides = []
        for s in (2 * p, 2 * p + 1):
            group = ask_ref[s, :, cap : 2 * cap]
            parts = [grad_ref[s], rest_ref[s], jnp.zeros((16 - CH, cap), F32)]
            grad = jnp.concatenate(parts, axis=0)
            wides.append(jnp.concatenate([jnp.where(group == k, grad, 0.0) for k in range(8)], axis=0))
        lines = [jnp.transpose(wide) for wide in wides]
        at = pl.ds(pl.multiple_of(p * 2 * share, 2 * share), 2 * share)
        for bank in banks:
            bank[at, :] = jnp.zeros((2 * share, 128), F32)
        for k, line in enumerate(lines):
            wide_ref[pl.ds(pl.multiple_of((2 * p + k) * cap, cap), cap), :] = line

    @pl.loop(0, devices)
    def _(s):
        base = s * (line_ref.shape[0] // devices)

        @pl.loop(0, (line_ref[base + 2 * cap] + burst - 1) // burst)
        def _(j):
            first = j * burst
            lines = wide_ref.at[pl.ds(pl.multiple_of(s * cap + first, burst), burst), :]
            for u in range(burst):
                bank = banks[u % len(banks)]
                at = pl.ds(line_ref[base + first + u], 1)
                bank[at, :] = bank[at, :] + lines[u : u + 1, :]

    def leave(j):
        to = pl.ds(pl.multiple_of(j * 8 * BLOCK, 8 * BLOCK), 8 * BLOCK)
        return pltpu.make_async_copy(out_ref.at[:, to], out_hbm.at[:, to], out_sem)

    @pl.loop(0, rows // BLOCK, unroll=2)
    def _(j):
        at = pl.ds(pl.multiple_of(j * BLOCK, BLOCK), BLOCK)
        total = banks[0][at, :]
        for bank in banks[1:]:
            total = total + bank[at, :]
        turned = jnp.transpose(total)
        for k in range(8):
            to = pl.ds(pl.multiple_of((j * 8 + k) * BLOCK, BLOCK), BLOCK)
            out_ref[:, to] = turned[k * 16 : k * 16 + CH]
        leave(j).start()

    pltpu.make_async_copy(out_ref, out_hbm, out_sem).wait()


def body(splat_params, list_owner, list_slot, list_length, target):
    devices = lax.axis_size(("row", "col"))
    tiles, slots = list_slot.shape
    entries = tiles * slots
    splats = splat_params.shape[1]
    pixels = target.shape[2]
    cap = 2 * entries // devices
    total = devices * cap
    rows = splats // 8
    smem = pl.BlockSpec(memory_space=pltpu.SMEM)
    vmem = pl.BlockSpec(memory_space=pltpu.VMEM)
    rendered, asked, incoming, coming = pl.pallas_call(
        step_kernel,
        in_specs=[smem, vmem, vmem, vmem, pl.BlockSpec(memory_space=pl.ANY)],
        out_specs=(vmem, vmem, vmem, vmem),
        out_shape=(
            jax.ShapeDtypeStruct((4, tiles, pixels), F32),
            jax.ShapeDtypeStruct((devices, 1, 2 * cap + 128), jnp.int32),
            jax.ShapeDtypeStruct((devices, 8, cap), F32),
            jax.ShapeDtypeStruct((devices, CH - 8, cap), F32),
        ),
        scratch_shapes=[
            pltpu.VMEM((CH, splats), F32),
            pltpu.VMEM((rows, 128), F32),
            pltpu.VMEM((128, BLOCK), F32),
            pltpu.VMEM((cap, 128), F32),
            pltpu.VMEM((cap, 128), F32),
            pltpu.SMEM((devices, 1, 2 * cap + 128), jnp.int32),
            pltpu.VMEM((tiles, 1, slots), jnp.int32),
            pltpu.VMEM((tiles, 1, slots), jnp.int32),
            pltpu.VMEM((devices, 1, 2 * cap + 128), jnp.int32),
            pltpu.VMEM((devices, 8, cap), F32),
            pltpu.VMEM((devices, CH - 8, cap), F32),
            pltpu.VMEM((devices, 8, cap), F32),
            pltpu.VMEM((devices, CH - 8, cap), F32),
            pltpu.VMEM((devices, 8, cap), F32),
            pltpu.VMEM((devices, CH - 8, cap), F32),
            pltpu.VMEM((CH * devices, 2 * cap), BF16),
            pltpu.VMEM((CH * devices, cap), F32),
            pltpu.VMEM((16, slots), F32),
            pltpu.VMEM((16, slots), F32),
            pltpu.VMEM((pixels, slots), F32),
            pltpu.VMEM((pixels, slots), F32),
            pltpu.VMEM((pixels, 2 * SB), BF16),
            pltpu.VMEM((pixels, SB), F32),
            pltpu.VMEM((pixels, SB), F32),
            pltpu.VMEM((CH * devices, 2 * slots), BF16),
            pltpu.VMEM((pixels, slots), BF16),
            pltpu.VMEM((pixels, slots), BF16),
            pltpu.SemaphoreType.DMA((2,)),
            pltpu.SemaphoreType.DMA((5,)),
            pltpu.SemaphoreType.DMA((5,)),
        ],
        compiler_params=pltpu.CompilerParams(collective_id=0, has_side_effects=True),
        name="step",
    )(list_length, list_owner.reshape(tiles, 1, slots), list_slot, target, splat_params)
    splat_grads = pl.pallas_call(
        scatter_kernel,
        in_specs=[smem, vmem, vmem, vmem],
        out_specs=pl.BlockSpec(memory_space=pl.ANY),
        out_shape=jax.ShapeDtypeStruct((CH, splats), F32),
        scratch_shapes=[
            pltpu.VMEM((total, 128), F32),
            pltpu.VMEM((CH, splats), F32),
            pltpu.SemaphoreType.DMA,
        ]
        + [pltpu.VMEM((rows, 128), F32)] * 4,
        name="accumulate",
    )(asked.reshape(-1), asked, incoming, coming)
    return (rendered, splat_grads)


def solution(mesh):
    in_specs = (
        P(None, ("row", "col")),
        P(("row", "col"), None, None),
        P(("row", "col"), None),
        P(("row", "col")),
        P(None, ("row", "col"), None),
    )
    out_specs = (P(None, ("row", "col"), None), P(None, ("row", "col")))
    return jax.shard_map(body, mesh=mesh, in_specs=in_specs, out_specs=out_specs, check_vma=False)
```

profile of v0, /device:TPU:19, one launch (start us, length us, event | category | flops | bytes accessed | tf_op | source)
XLA Modules:
  0.0 69.7 jit_solution(2001813024566671274)
XLA Ops:
  0.6 52.0 %step.1 = (f32[4,4,256]{2,1,0:T(4,128)}, s32[32,1,640]{2,1,0:T(1,128)}, f32[32,8,256]{2,1,0:T(8,128)}, f32[32,2,256]{2,1,0:T(2,128)}) custom-call(s32[4]{0:T(128)} %length_ref.1, s32[4,1,1024]{2,1,0:T(1,128)} %bitcast.3, s32[4,1024]{1,0:T(4,128)} %slot_ref.1, f32[4,4,256]{2,1,0:T(4,128)} %target_ref.1, f32[10,65536]{1,0:T(8,128)} %params_hbm.1), custom_call_target="tpu_custom_call" | custom-call | tf_op jit(solution)/shard_map/step/pallas_call | solution.py:384
  52.7 0.0 copy-start
  52.7 16.4 %accumulate.1 = f32[10,65536]{1,0:T(8,128)} custom-call(s32[20480]{0:T(1024)} %bitcast.2, s32[32,1,640]{2,1,0:T(1,128)} %get-tuple-element.7.ask_ref, f32[32,8,256]{2,1,0:T(8,128)} %get-tuple-element.8.grad_ref, f32[32,2,256]{2,1,0:T(2,128)} %get-tuple-element.9.rest_ref), custom_call_target="tpu_custom_call" | custom-call | tf_op jit(solution)/shard_map/accumulate/pallas_call | solution.py:429
  69.1 0.0 copy-done
  69.1 0.6 copy.8
Async XLA Ops:
  52.7 16.4 %copy-start = (f32[4,4,256]{2,1,0:T(4,128)S(1)}, f32[4,4,256]{2,1,0:T(4,128)}, u32[]{:S(2)}) copy-start(f32[4,4,256]{2,1,0:T(4,128)} %get-tuple-element.12) | copy-start | bytes 49156
where the time goes:
time: 70.5 us; the launch traced here: 69.7 us
  Pallas kernels  68.5 us (97%)
    pallas_call x1, Pallas kernels, body(): pl.pallas_call(step_kernel, in_specs=[smem, vmem, vmem, vmem, pl.BlockSpe...  52 us
    pallas_call x1, Pallas kernels, body(): pl.pallas_call(scatter_kernel, in_specs=[smem, vmem, vmem, vmem], out_spe...  16.4 us

commit v1 on v0

--- a/solution.py
+++ b/solution.py
@@ -316,12 +316,13 @@
 
 
 def scatter_kernel(
-    line_ref, ask_ref, grad_ref, rest_ref, out_hbm, wide_ref, out_ref, out_sem, *banks
+    line_ref, ask_ref, grad_ref, rest_ref, seen_ref, image_ref, out_hbm, wide_ref, out_ref, out_sem, *banks
 ):
     rows = banks[0].shape[0]
     devices, _, cap = grad_ref.shape
     share = rows // devices
     burst = 32
+    image_ref[...] = seen_ref[...]
 
     @pl.loop(0, devices // 2)
     def _(p):
@@ -381,7 +382,7 @@
     rows = splats // 8
     smem = pl.BlockSpec(memory_space=pltpu.SMEM)
     vmem = pl.BlockSpec(memory_space=pltpu.VMEM)
-    rendered, asked, incoming, coming = pl.pallas_call(
+    seen, asked, incoming, coming = pl.pallas_call(
         step_kernel,
         in_specs=[smem, vmem, vmem, vmem, pl.BlockSpec(memory_space=pl.ANY)],
         out_specs=(vmem, vmem, vmem, vmem),
@@ -426,11 +427,14 @@
         compiler_params=pltpu.CompilerParams(collective_id=0, has_side_effects=True),
         name="step",
     )(list_length, list_owner.reshape(tiles, 1, slots), list_slot, target, splat_params)
-    splat_grads = pl.pallas_call(
+    rendered, splat_grads = pl.pallas_call(
         scatter_kernel,
-        in_specs=[smem, vmem, vmem, vmem],
-        out_specs=pl.BlockSpec(memory_space=pl.ANY),
-        out_shape=jax.ShapeDtypeStruct((CH, splats), F32),
+        in_specs=[smem, vmem, vmem, vmem, vmem],
+        out_specs=(vmem, pl.BlockSpec(memory_space=pl.ANY)),
+        out_shape=(
+            jax.ShapeDtypeStruct((4, tiles, pixels), F32),
+            jax.ShapeDtypeStruct((CH, splats), F32),
+        ),
         scratch_shapes=[
             pltpu.VMEM((total, 128), F32),
             pltpu.VMEM((CH, splats), F32),
@@ -438,7 +442,7 @@
         ]
         + [pltpu.VMEM((rows, 128), F32)] * 4,
         name="accumulate",
-    )(asked.reshape(-1), asked, incoming, coming)
+    )(asked.reshape(-1), asked, incoming, coming, seen)
     return (rendered, splat_grads)
 
 

time: 70.5 us -> 70.9 us (level)
  the two profiles are of different devices: /device:TPU:19 before, /device:TPU:28 now
where the time goes in v1:
time: 70.9 us; the launch traced here: 69.9 us
  Pallas kernels  69.3 us (98%)
    pallas_call x1, Pallas kernels, body(): pl.pallas_call(step_kernel, in_specs=[smem, vmem, vmem, vmem, pl.BlockSpe...  52.7 us
    pallas_call x1, Pallas kernels, body(): pl.pallas_call(scatter_kernel, in_specs=[smem, vmem, vmem, vmem, vmem], o...  16.6 us

profile of v1, /device:TPU:28, one launch (start us, length us, event | category | flops | bytes accessed | tf_op | source)
XLA Modules:
  0.0 69.9 jit_solution(6929111006871379646)
XLA Ops:
  0.6 52.7 %step.1 = (f32[4,4,256]{2,1,0:T(4,128)}, s32[32,1,640]{2,1,0:T(1,128)}, f32[32,8,256]{2,1,0:T(8,128)}, f32[32,2,256]{2,1,0:T(2,128)}) custom-call(s32[4]{0:T(128)} %length_ref.1, s32[4,1,1024]{2,1,0:T(1,128)} %bitcast.3, s32[4,1024]{1,0:T(4,128)} %slot_ref.1, f32[4,4,256]{2,1,0:T(4,128)} %target_ref.1, f32[10,65536]{1,0:T(8,128)} %params_hbm.1), custom_call_target="tpu_custom_call" | custom-call | tf_op jit(solution)/shard_map/step/pallas_call | solution.py:385
  53.3 16.6 %accumulate.1 = (f32[4,4,256]{2,1,0:T(4,128)}, f32[10,65536]{1,0:T(8,128)}) custom-call(s32[20480]{0:T(1024)} %bitcast.2, s32[32,1,640]{2,1,0:T(1,128)} %get-tuple-element.6.ask_ref, f32[32,8,256]{2,1,0:T(8,128)} %get-tuple-element.7.grad_ref, f32[32,2,256]{2,1,0:T(2,128)} %get-tuple-element.8.rest_ref, f32[4,4,256]{2,1,0:T(4,128)} %get-tuple-element.9.seen_ref), custom_call_target="tpu_custom_call" | custom-call | tf_op jit(solution)/shard_map/accumulate/pallas_call | solution.py:430
